TPU v7x, 128 devices: a whole 4x4x4 slice. The times are simulated.
128 devices in a mesh: col: 8 (over x, z_lo), row: 16 (over y, z_hi, core).
Axes of the slice: x: 4, y: 4, z: 4 (z_hi: 2, z_lo: 2; z = z_hi * 2 + z_lo), core: 2. Of those that a mesh axis runs over, the one named last changes fastest.
Arguments:
- covariance: float32 [12288, 12288], P('row', 'col'), may hold values from -2 to 2, as said below
- wfs_map: int32 [12288], P('row'), may hold values from 0 to 5
- noise_var: float32 [6], replicated, may hold values from 0.5 to 2
- targets: float32 [12288, 2048], P('row', 'col'), may hold values from -0.6 to 0.6
- target_pos: float32 [2, 2048], replicated, may hold values from -1 to 1
- layer_strength: float32 [35], replicated, may hold values from 0.005 to 0.05
- layer_scale: float32 [35], replicated, may hold values from 0.2 to 2
- tile_layer: int32 [16], replicated, may hold values from 0 to 34
Outputs:
- updated: float32 [12288, 12288], P('row', 'col')
- panel_factor: float32 [12288, 256], P('row')
- reconstructor: float32 [12288, 2048], P('row', 'col')
- error_cov: float32 [2048, 2048], P('row', 'col')
Inputs may be any that keep to these rules, and one draw needn't show every extreme that they name: `covariance`: symmetric and positive semidefinite; its diagonal lies between 0.5 and 2.
All inputs are finite; a program needn't handle non-finite values.
Results may differ from a plain program's by a relative error of at most 0.0003.
Values sent between devices are 32-bit elements; how exact they have to be, the bound alone decides.
No kernel may reach another device: no remote copies, remote signals or barrier semaphores. Data moves between devices by JAX's collectives and lax.ppermute only.
A program may use at most 64 MiB of HBM per device.

v0:
```python
import jax
import jax.numpy as jnp
from jax import lax
from jax.sharding import PartitionSpec as P

PB = 256
TILE = 128
precise = lax.Precision.HIGHEST


def broadcast(shard, axis, root):
    mine = lax.axis_index(axis) == root
    return lax.psum(jnp.where(mine, shard, jnp.zeros_like(shard)), axis)


def lookup(values, indices, entries):
    one_hot = (indices[:, None] == jnp.arange(entries, dtype=jnp.int32)[None, :]).astype(
        jnp.float32
    )
    return jnp.dot(one_hot, values, precision=precise)


def target_covariance(pos_rows, pos_cols, layer_rows, layer_cols, layer_strength, layer_scale):
    distance = (pos_rows[0][:, None] - pos_cols[0][None, :]) ** 2 + (
        pos_rows[1][:, None] - pos_cols[1][None, :]
    ) ** 2
    lowest = jnp.minimum(layer_rows[:, None], layer_cols[None, :])
    levels = jnp.arange(layer_strength.shape[0], dtype=jnp.int32)
    weights = layer_strength[:, None, None] / (
        1.0 + distance[None] / (layer_scale * layer_scale)[:, None, None]
    )
    return jnp.sum(jnp.where(levels[:, None, None] <= lowest[None], weights, 0.0), axis=0)


def local(
    covariance, wfs_map, noise_var, targets, target_pos, layer_strength, layer_scale, tile_layer
):
    row_count, col_count = covariance.shape
    target_width = targets.shape[1]
    row_index = lax.axis_index("row")
    col_index = lax.axis_index("col")
    row_ids = row_index * row_count + jnp.arange(row_count, dtype=jnp.int32)
    col_ids = col_index * col_count + jnp.arange(col_count, dtype=jnp.int32)
    noise_rows = lookup(noise_var, wfs_map, noise_var.shape[0])
    on_diagonal = row_ids[:, None] == col_ids[None, :]
    matrix = covariance + jnp.where(on_diagonal, noise_rows[:, None], 0.0)
    diag_block = broadcast(matrix[:PB, :PB], ("col", "row"), 0)
    factor = jnp.linalg.cholesky(diag_block)
    solved = jax.scipy.linalg.solve_triangular(factor, matrix[:, :PB].T, lower=True).T
    top_rows = jnp.concatenate([factor, jnp.zeros((row_count - PB, PB), jnp.float32)], axis=0)
    own_rows = jnp.where(row_ids[:, None] < PB, top_rows, solved)
    panel_rows = broadcast(own_rows, "col", 0)
    head_rows = jax.scipy.linalg.solve_triangular(factor, targets[:PB], lower=True)
    upper_rows = jax.scipy.linalg.solve_triangular(factor, matrix[:PB, :], lower=True)
    lead_cols = jnp.concatenate([factor.T, jnp.zeros((PB, col_count - PB), jnp.float32)], axis=1)
    upper_rows = jnp.where(col_ids[None, :] < PB, lead_cols, upper_rows)
    upper_rows, head_cols = (broadcast(upper_rows, "row", 0), broadcast(head_rows, "row", 0))
    product = jnp.dot(panel_rows, upper_rows, precision=precise)
    fill_cols = jnp.concatenate(
        [panel_rows, jnp.zeros((row_count, col_count - PB), jnp.float32)], axis=1
    )
    trailing = (row_ids[:, None] >= PB) & (col_ids[None, :] >= PB)
    updated = jnp.where(
        trailing, matrix - product, jnp.where(col_ids[None, :] < PB, fill_cols, 0.0)
    )
    head_top = jnp.concatenate(
        [head_cols, jnp.zeros((row_count - PB, target_width), jnp.float32)], axis=0
    )
    reduced = targets - jnp.dot(panel_rows, head_cols, precision=precise)
    reconstructor = jnp.where(row_ids[:, None] < PB, head_top, reduced)
    error_rows = target_width * lax.axis_size("col") // lax.axis_size("row")
    row_start = row_index * error_rows
    gathered = lax.all_gather(head_cols, "col", axis=1, tiled=True)
    head_needed = lax.dynamic_slice_in_dim(gathered, row_start, error_rows, 1)
    layer_all = jnp.repeat(tile_layer, TILE)
    col_start = col_index * target_width
    pos_rows = lax.dynamic_slice_in_dim(target_pos, row_start, error_rows, 1)
    pos_cols = lax.dynamic_slice_in_dim(target_pos, col_start, target_width, 1)
    layer_rows = lax.dynamic_slice_in_dim(layer_all, row_start, error_rows, 0)
    layer_cols = lax.dynamic_slice_in_dim(layer_all, col_start, target_width, 0)
    target_cov = target_covariance(
        pos_rows, pos_cols, layer_rows, layer_cols, layer_strength, layer_scale
    )
    error_cov = target_cov - lax.dot_general(
        head_needed,
        head_cols,
        (((0,), (0,)), ((), ())),
        precision=precise,
        preferred_element_type=jnp.float32,
    )
    return (updated, panel_rows, reconstructor, error_cov)


def solution(mesh):
    placed = (P("row", "col"), P("row"), P(), P("row", "col"), P(), P(), P(), P())
    return jax.shard_map(
        local,
        mesh=mesh,
        in_specs=placed,
        out_specs=(P("row", "col"), P("row", None), P("row", "col"), P("row", "col")),
        check_vma=False,
    )
```

profile of v0, /device:TPU:0, one launch (start us, length us, event | category | flops | bytes accessed | tf_op | source)
XLA Modules:
  0.0 518.4 jit_solution(5108484847680421361)
XLA Ops:
  7.2 0.0 all-reduce.10.cloned.1.call-start
  7.2 6.1 %copy.26 = f32[768,1536]{0,1:T(8,128)} copy(f32[768,1536]{1,0:T(8,128)} %param.8) | data formatting | bytes 9437184 | tf_op args[0]
  13.3 0.4 convolution_reduce_fusion
  13.8 2.9 select_add_fusion
  16.6 2.2 copy-done.1
  18.8 0.7 slice_select_fusion
  19.5 0.0 all-reduce.10.cloned.1.call-update
  19.6 0.0 all-reduce.14.cloned.1.call-start
  19.7 144.5 %all-reduce.10.cloned.1.call-done = f32[256,256]{0,1:T(8,128)} async-done(((f32[256,256]{0,1:T(8,128)}), f32[256,256]{0,1:T(8,128)}) %all-reduce.10.cloned.1.call-update) | async-done | bytes 262160 | tf_op jit(solution)/shard_map/psum | solution.py:13
  164.2 1.1 copy.27
  165.2 1.0 fusion.11
  166.3 11.7 %cholesky.49 = f32[128,128]{1,0:T(8,128)S(1)} custom-call(f32[128,128]{1,0:T(8,128)S(1)} %cholesky.115), custom_call_target="Cholesky" | custom-call | tf_op jit(solution)/shard_map/jit(cholesky)/cholesky | solution.py:48
  178.0 0.1 copy.28
  178.1 9.8 %custom-call.21 = f32[1,128,128]{1,2,0:T(8,128)S(1)} custom-call(f32[1,128,128]{2,1,0:T(8,128)S(1)} %get-tuple-element.43), custom_call_target="InvertDiagBlocksLowerTriangular" | custom-call | tf_op jit(solution)/shard_map/jit(cholesky)/cholesky | solution.py:48
  187.9 0.2 fusion.17
  188.1 0.1 copy.29
  188.2 0.3 convolution_subtract_fusion.5
  188.5 11.7 %cholesky.103 = f32[128,128]{1,0:T(8,128)S(1)} custom-call(f32[128,128]{1,0:T(8,128)S(1)} %convolution_subtract_fusion.5), custom_call_target="Cholesky" | custom-call | tf_op jit(solution)/shard_map/jit(cholesky)/cholesky | solution.py:48
  200.2 0.1 copy.30
  200.4 0.6 compare_reduce_fusion
  202.4 0.1 triangular_solve.72
  202.5 4.4 while.1
  202.6 0.6 fusion.47
  203.2 1.4 dynamic-slice.11
  204.6 0.1 copy.45
  204.7 0.6 fusion.47
  205.3 1.4 dynamic-slice.11
  206.7 0.1 copy.45
  206.8 19.7 %custom-call.22 = f32[2,128,128]{1,2,0:T(8,128)S(1)} custom-call(f32[2,128,128]{2,1,0:T(8,128)S(1)} %get-tuple-element.11), custom_call_target="InvertDiagBlocksLowerTriangular" | custom-call | tf_op jit(solution)/shard_map/jit(_solve_triangular)/triangular_solve | solution.py:49
  226.5 2.0 fusion.5
  228.5 1.2 fusion.15
  229.8 1.2 convolution_subtract_fusion.4
  231.0 0.1 copy.33
  231.1 2.5 convolution_subtract_fusion
  233.6 0.9 fusion.21
  234.5 0.4 fusion.20
  234.9 0.7 maximum_select_fusion.1
  235.6 1.3 fusion.3
  237.0 0.0 all-reduce.14.cloned.1.call-update
  237.0 0.0 all-reduce.12.cloned.1.call-start
  237.1 1.2 slice_bitcast_fusion
  238.3 0.5 fusion.9
  238.9 0.5 convolution_subtract_fusion.2
  239.4 0.5 fusion.22
  239.9 1.0 fusion.8
  240.9 0.0 all-gather.2.cloned.1.call-start
  240.9 137.2 %all-reduce.14.cloned.1.call-done = (f32[256,1536]{1,0:T(8,128)}, f32[256,256]{0,1:T(8,128)}) async-done(((f32[256,1536]{1,0:T(8,128)}, f32[256,256]{0,1:T(8,128)}), (f32[256,1536]{1,0:T(8,128)}, f32[256,256]{0,1:T(8,128)})) %all-reduce.14.cloned.1.call-update) | async-done | bytes 1835024 | tf_op jit(solution)/shard_map/psum | solution.py:13
  378.1 0.3 copy.35
  378.5 0.1 broadcast_bitcast_fusion
  378.5 0.1 dynamic_slice.16
  378.6 0.1 dynamic_slice.15
  378.7 0.7 constant_dynamic-slice_fusion.2
  379.4 0.8 constant_dynamic-slice_fusion.1
  380.2 0.1 broadcast_minimum_fusion
  380.3 0.1 multiply_add_fusion
  380.4 1.2 fusion.2
  381.6 76.2 %all-reduce.12.cloned.1.call-done = f32[768,256]{0,1:T(8,128)} async-done(((f32[768,256]{0,1:T(8,128)}), f32[768,256]{0,1:T(8,128)}) %all-reduce.12.cloned.1.call-update) | async-done | bytes 786448 | tf_op jit(solution)/shard_map/psum | solution.py:13
  457.8 2.3 copy.38
  460.1 9.2 %select_select_fusion = f32[768,1536]{0,1:T(8,128)} fusion(f32[768,256]{0,1:T(8,128)} %all-reduce.12.cloned.1.call-done, f32[768,1536]{0,1:T(8,128)} %copy-done.1, f32[256,1536]{1,0:T(8,128)S(1)} %copy-done.4, pred[1536]{0:T(1024)(128)(4,1)S(1)} %fusion.26, pred[768]{0:T(1024)(128)(4,1)S(1)} %fusion.29, pred[1536]{0:T(1024)(128)(4,1)S(1)} %fusion.27), kind=kOutput, calls=%fused_computation.2 | convolution fusion | flops 3628597248 | bytes 11800320 | tf_op jit(solution)/shard_map/dot_general | solution.py:58
  469.3 6.1 %copy.37 = f32[768,1536]{1,0:T(8,128)} copy(f32[768,1536]{0,1:T(8,128)} %select_select_fusion) | data formatting | bytes 9437184
  475.4 0.9 fusion.4
  476.3 1.1 copy.39
  477.5 32.4 %all-gather.2.cloned.1.call-done = f32[256,2048]{0,1:T(8,128)} async-done(((f32[256,256]{0,1:T(8,128)}), f32[256,2048]{0,1:T(8,128)}) %all-gather.2.cloned.1.call-update) | async-done | bytes 2097168 | tf_op jit(solution)/shard_map/all_gather | solution.py:73
  509.9 2.0 convolution_subtract_fusion.3
  (42 shorter events, 0.3 us)
Async XLA Ops:
  7.2 371.3 %copy-start = (s32[16]{0:T(128)S(1)}, s32[16]{0:T(128)}, u32[]{:S(2)}) copy-start(s32[16]{0:T(128)} %param.15) | copy-start | bytes 196
  7.2 157.0 %all-reduce.10.cloned.1.call-start = ((), (), s32[]{:S(2)}) async-start(), calls=%async_computation | async-start | bytes 524288 | tf_op jit(solution)/shard_map/psum | solution.py:13
  7.2 6.1 %copy-start.7 = (s32[768]{0:T(1024)S(1)}, s32[768]{0:T(1024)}, u32[]{:S(2)}) copy-start(s32[768]{0:T(1024)} %param.9) | copy-start | bytes 9220
  7.2 6.1 %copy-start.8 = (f32[6]{0:T(128)S(1)}, f32[6]{0:T(128)}, u32[]{:S(2)}) copy-start(f32[6]{0:T(128)} %param.10) | copy-start | bytes 76
  16.6 2.2 copy-start.1
  19.6 358.5 %all-reduce.14.cloned.1.call-start = ((), (), s32[]{:S(2)}) async-start(), calls=%async_computation.3 | async-start | bytes 3670016 | tf_op jit(solution)/shard_map/psum | solution.py:13
  237.0 141.2 %copy-start.5 = (f32[768,256]{1,0:T(8,128)S(1)}, f32[768,256]{1,0:T(8,128)}, u32[]{:S(2)}) copy-start(f32[768,256]{1,0:T(8,128)} %param.11) | copy-start | bytes 2359300
  237.0 141.4 %copy-start.9 = (f32[35]{0:T(128)S(1)}, f32[35]{0:T(128)}, u32[]{:S(2)}) copy-start(f32[35]{0:T(128)} %param.14) | copy-start | bytes 424
  237.0 220.8 %all-reduce.12.cloned.1.call-start = ((), (), s32[]{:S(2)}) async-start(), calls=%async_computation.1 | async-start | bytes 1572864 | tf_op jit(solution)/shard_map/psum | solution.py:13
  237.1 143.3 %copy-start.6 = (f32[35]{0:T(128)S(1)}, f32[35]{0:T(128)}, u32[]{:S(2)}) copy-start(f32[35]{0:T(128)} %param.13) | copy-start | bytes 424
  240.9 269.0 %all-gather.2.cloned.1.call-start = ((), (), s32[]{:S(2)}) async-start(), calls=%async_computation.2 | async-start | bytes 2359296 | tf_op jit(solution)/shard_map/all_gather | solution.py:73
  378.1 82.0 %copy-start.4 = (f32[256,1536]{1,0:T(8,128)S(1)}, f32[256,1536]{1,0:T(8,128)}, u32[]{:S(2)}) copy-start(f32[256,1536]{1,0:T(8,128)} %get-tuple-element.36) | copy-start | bytes 4718596
  469.3 6.1 %copy-start.2 = (f32[768,256]{0,1:T(8,128)S(1)}, f32[768,256]{0,1:T(8,128)}, u32[]{:S(2)}) copy-start(f32[768,256]{0,1:T(8,128)} %all-reduce.12.cloned.1.call-done) | copy-start | bytes 2359300
  469.3 6.1 %copy-start.3 = (f32[256,256]{0,1:T(8,128)S(1)}, f32[256,256]{0,1:T(8,128)}, u32[]{:S(2)}) copy-start(f32[256,256]{0,1:T(8,128)} %get-tuple-element.37) | copy-start | bytes 786436
Sparse Core Ops, SparseCore 0:
  19.7 144.4 all-reduce.9
  237.1 140.9 all-reduce.13
  381.3 76.4 all-reduce.11
  459.3 50.5 all-gather.1
where the time goes:
time: 519 us; the launch traced here: 518 us
  waiting for transfers between devices  390 us (75%)
  other arithmetic  62.7 us (12%)
  local copies, waits for them, and re-layouts  26.8 us (5%)
  matrix products  22.7 us (4%)
  between operations  15.5 us (3%)
    psum x3, waiting for transfers between devices, broadcast(): return lax.psum(jnp.where(mine, shard, jnp.zeros_like(shard)), axis)  358 us
    another operation x6, other arithmetic, local(): factor = jnp.linalg.cholesky(diag_block)  33.9 us
    all_gather x1, waiting for transfers between devices, local(): gathered = lax.all_gather(head_cols, 'col', axis=1, tiled=True)  32.4 us
    another operation x3, other arithmetic, local(): jax.scipy.linalg.solve_triangular(factor, matrix[:, :PB].T, lower=True)  19.7 us
    unnamed x25, local copies, waits for them, and re-layouts  18.1 us
  transfers between devices with their start and end apart: 4, of which 4 were waited for; matrix products, arithmetic and copies ran while one was open for 5% of the time, Pallas kernels for 0%

commit v1 on v0

--- a/solution.py
+++ b/solution.py
@@ -10,7 +10,7 @@
 
 def broadcast(shard, axis, root):
     mine = lax.axis_index(axis) == root
-    return lax.psum(jnp.where(mine, shard, jnp.zeros_like(shard)), axis)
+    return jnp.sum(lax.all_gather(jnp.where(mine, shard, jnp.zeros_like(shard)), axis), axis=0)
 
 
 def lookup(values, indices, entries):

time: 519 us -> 776 us (1.50)
  waiting for transfers between devices: 390 us -> 623 us
  other arithmetic: 62.7 us -> 90.5 us
    all_gather x0 -> x4, waiting for transfers between devices: none -> 574 us  [broadcast(): lax.all_gather(jnp.where(mine, shard, jnp.zeros_like(shard)), axis)]
    psum x3 -> x0, waiting for transfers between devices: 358 us -> none  [broadcast(): return lax.psum(jnp.where(mine, shard, jnp.zeros_like(shard)), axis)]
    reduce_sum x0 -> x4, other arithmetic: none -> 28.3 us  [broadcast(): jnp.sum(lax.all_gather(jnp.where(mine, shard, jnp.zeros_like(shard)), axi...]
    all_gather x1, waiting for transfers between devices: 32.4 us -> 49.3 us  [local(): gathered = lax.all_gather(head_cols, 'col', axis=1, tiled=True)]
    unnamed x25 -> x21, local copies, waits for them, and re-layouts: 18.1 us -> 17.8 us
  transfers between devices with their start and end apart: 4 -> 5, of which waited for: 4 -> 5; matrix products, arithmetic and copies ran while one was open for 5% -> 3% of each run, Pallas kernels for 0% -> 0%
where the time goes in v1:
time: 776 us; the launch traced here: 774 us
  waiting for transfers between devices  623 us (80%)
  other arithmetic  90.5 us (12%)
  local copies, waits for them, and re-layouts  25.3 us (3%)
  matrix products  19.4 us (2%)
  between operations  15.5 us (2%)
    all_gather x4, waiting for transfers between devices, broadcast(): lax.all_gather(jnp.where(mine, shard, jnp.zeros_like(shard)), axis)  574 us
    all_gather x1, waiting for transfers between devices, local(): gathered = lax.all_gather(head_cols, 'col', axis=1, tiled=True)  49.3 us
    another operation x6, other arithmetic, local(): factor = jnp.linalg.cholesky(diag_block)  33.9 us
    reduce_sum x4, other arithmetic, broadcast(): jnp.sum(lax.all_gather(jnp.where(mine, shard, jnp.zeros_like(shard)), axi...  28.3 us
    another operation x3, other arithmetic, local(): jax.scipy.linalg.solve_triangular(factor, matrix[:, :PB].T, lower=True)  19.9 us
    unnamed x21, local copies, waits for them, and re-layouts  17.8 us
  transfers between devices with their start and end apart: 5, of which 5 were waited for; matrix products, arithmetic and copies ran while one was open for 3% of the time, Pallas kernels for 0%

profile of v1, /device:TPU:0, one launch (start us, length us, event | category | flops | bytes accessed | tf_op | source)
XLA Modules:
  0.0 774.1 jit_solution(9073733264702323311)
XLA Ops:
  7.2 0.0 all-gather.13.cloned.1.call-start
  7.3 1.1 convolution_reduce_fusion
  8.4 2.9 select_add_fusion
  11.3 2.2 copy-done.2
  13.5 0.7 slice_select_fusion
  14.2 0.0 all-gather.13.cloned.1.call-update
  14.2 0.0 all-gather.9.cloned.1.call-start
  14.3 240.1 %all-gather.13.cloned.1.call-done = f32[32768,256]{1,0:T(8,128)} async-done(((f32[256,256]{1,0:T(8,128)}), f32[32768,256]{1,0:T(8,128)}) %all-gather.13.cloned.1.call-update) | async-done | bytes 33554448 | tf_op jit(solution)/shard_map/all_gather | solution.py:13
  254.4 12.0 %reduce_sum.45 = f32[256,256]{1,0:T(8,128)S(1)} reduce(f32[128,256,256]{2,1,0:T(8,128)} %bitcast.74, f32[]{:T(128)} %constant.121.clone.1), dimensions={0}, to_apply=%region_0.1 | reduce | flops 8323072 | bytes 33816580 | tf_op jit(solution)/shard_map/reduce_sum | solution.py:13
  266.4 0.1 copy.22
  266.6 11.7 %cholesky.49 = f32[128,128]{1,0:T(8,128)S(1)} custom-call(f32[128,128]{1,0:T(8,128)S(1)} %cholesky.115), custom_call_target="Cholesky" | custom-call | tf_op jit(solution)/shard_map/jit(cholesky)/cholesky | solution.py:48
  278.4 9.8 %custom-call.21 = f32[1,128,128]{1,2,0:T(8,128)S(1)} custom-call(f32[1,128,128]{2,1,0:T(8,128)S(1)} %get-tuple-element.27), custom_call_target="InvertDiagBlocksLowerTriangular" | custom-call | tf_op jit(solution)/shard_map/jit(cholesky)/cholesky | solution.py:48
  288.2 0.2 constant_dynamic-update-slice_fusion
  288.4 0.3 convolution_subtract_fusion.5
  288.7 11.7 %cholesky.103 = f32[128,128]{1,0:T(8,128)S(1)} custom-call(f32[128,128]{1,0:T(8,128)S(1)} %convolution_subtract_fusion.5), custom_call_target="Cholesky" | custom-call | tf_op jit(solution)/shard_map/jit(cholesky)/cholesky | solution.py:48
  300.5 0.6 compare_reduce_fusion
  302.4 0.1 triangular_solve.76
  302.5 4.0 while.1
  302.5 0.6 fusion.46
  303.1 1.4 bitcast_dynamic-update-slice_fusion.2
  304.5 0.6 fusion.46
  305.1 1.4 bitcast_dynamic-update-slice_fusion.2
  306.5 19.9 %custom-call.22 = f32[2,128,128]{1,2,0:T(8,128)S(1)} custom-call(f32[2,128,128]{2,1,0:T(8,128)S(1)} %get-tuple-element.11), custom_call_target="InvertDiagBlocksLowerTriangular" | custom-call | tf_op jit(solution)/shard_map/jit(_solve_triangular)/triangular_solve | solution.py:49
  326.4 0.3 fusion.15
  326.7 0.3 convolution_subtract_fusion.4
  327.0 0.3 convolution_bitcast_fusion
  327.3 0.7 maximum_select_fusion.1
  328.0 0.0 all-gather.9.cloned.1.call-update
  328.0 0.0 all-gather.15.cloned.1.call-start
  328.1 1.2 slice_bitcast_fusion
  329.3 0.5 fusion.9
  329.8 0.2 copy.24
  330.0 0.8 convolution_subtract_fusion.2
  330.8 0.5 fusion.21
  331.3 1.1 fusion.8
  332.3 0.0 all-gather.15.cloned.1.call-update
  332.3 0.0 all-gather.11.cloned.1.call-start
  332.4 50.0 %all-gather.9.cloned.1.call-done = f32[16,256,256]{2,1,0:T(8,128)} async-done(((f32[1,256,256]{2,1,0:T(8,128)}), f32[16,256,256]{2,1,0:T(8,128)}) %all-gather.9.cloned.1.call-update) | async-done | bytes 4194320 | tf_op jit(solution)/shard_map/all_gather | solution.py:13
  382.4 3.2 reduce_sum.48
  385.6 0.0 all-gather.11.cloned.1.call-update
  385.6 0.0 all-gather.17.cloned.1.call-start
  385.7 2.0 fusion.5
  387.7 0.3 copy.26
  387.9 1.9 convolution_subtract_fusion
  389.9 1.4 fusion.20
  391.3 1.5 fusion.3
  392.7 0.0 all-gather.17.cloned.1.call-update
  392.8 0.1 broadcast_bitcast_fusion
  392.9 0.1 dynamic_slice.16
  393.0 0.1 dynamic_slice.15
  393.0 0.7 constant_dynamic-slice_fusion.2
  393.7 0.8 constant_dynamic-slice_fusion.1
  394.6 0.1 broadcast_minimum_fusion
  394.6 0.1 multiply_add_fusion
  394.8 1.2 fusion.2
  395.9 116.4 %all-gather.15.cloned.1.call-done = f32[6144,256]{1,0:T(8,128)} async-done(((f32[768,256]{1,0:T(8,128)}), f32[6144,256]{1,0:T(8,128)}) %all-gather.15.cloned.1.call-update) | async-done | bytes 6291472 | tf_op jit(solution)/shard_map/all_gather | solution.py:13
  512.4 3.3 reduce_sum.46
  515.7 1.7 fusion.4
  517.4 49.3 %all-gather.11.cloned.1.call-done = f32[256,2048]{1,0:T(8,128)} async-done(((f32[256,256]{1,0:T(8,128)}), f32[256,2048]{1,0:T(8,128)}) %all-gather.11.cloned.1.call-update) | async-done | bytes 2097168 | tf_op jit(solution)/shard_map/all_gather | solution.py:73
  566.6 2.0 convolution_subtract_fusion.3
  568.6 167.3 %all-gather.17.cloned.1.call-done = f32[4096,1536]{0,1:T(8,128)} async-done(((f32[256,1536]{0,1:T(8,128)}), f32[4096,1536]{0,1:T(8,128)}) %all-gather.17.cloned.1.call-update) | async-done | bytes 25165840 | tf_op jit(solution)/shard_map/all_gather | solution.py:13
  735.9 15.6 %copy.31 = f32[192,8,16,256]{3,2,1,0:T(8,128)S(1)} copy(f32[192,8,16,256]{3,1,2,0:T(8,128)} %bitcast.77) | data formatting | bytes 50331648
  751.5 9.8 %bitcast_reduce_fusion = f32[256,1536]{0,1:T(8,128)S(1)} fusion(f32[192,8,16,256]{3,2,1,0:T(8,128)S(1)} %copy.31), kind=kLoop, calls=%fused_computation.2 | loop fusion | flops 5898240 | bytes 26738688 | tf_op jit(solution)/shard_map/reduce_sum | solution.py:13
  761.3 6.3 select_select_fusion
  (38 shorter events, 0.3 us)
Async XLA Ops:
  7.2 385.6 %copy-start = (s32[16]{0:T(128)S(1)}, s32[16]{0:T(128)}, u32[]{:S(2)}) copy-start(s32[16]{0:T(128)} %param.15) | copy-start | bytes 196
  7.2 247.2 %all-gather.13.cloned.1.call-start = ((), (), s32[]{:S(2)}) async-start(), calls=%async_computation.2 | async-start | bytes 33816576 | tf_op jit(solution)/shard_map/all_gather | solution.py:13
  11.3 2.2 copy-start.2
  14.2 368.2 %all-gather.9.cloned.1.call-start = ((), (), s32[]{:S(2)}) async-start(), calls=%async_computation | async-start | bytes 4456448 | tf_op jit(solution)/shard_map/all_gather | solution.py:13
  254.4 72.0 %copy-start.5 = (f32[768,256]{1,0:T(8,128)S(1)}, f32[768,256]{1,0:T(8,128)}, u32[]{:S(2)}) copy-start(f32[768,256]{1,0:T(8,128)} %param.11) | copy-start | bytes 2359300
  328.0 184.3 %all-gather.15.cloned.1.call-start = ((), (), s32[]{:S(2)}) async-start(), calls=%async_computation.3 | async-start | bytes 7077888 | tf_op jit(solution)/shard_map/all_gather | solution.py:13
  332.3 234.3 %all-gather.11.cloned.1.call-start = ((), (), s32[]{:S(2)}) async-start(), calls=%async_computation.1 | async-start | bytes 2359296 | tf_op jit(solution)/shard_map/all_gather | solution.py:73
  385.6 350.3 %all-gather.17.cloned.1.call-start = ((), (), s32[]{:S(2)}) async-start(), calls=%async_computation.4 | async-start | bytes 26738688 | tf_op jit(solution)/shard_map/all_gather | solution.py:13
  387.9 4.9 copy-start.7
  387.9 6.8 copy-start.6
  392.7 122.9 %copy-start.4 = (f32[256,256]{1,0:T(8,128)S(1)}, f32[256,256]{1,0:T(8,128)}, u32[]{:S(2)}) copy-start(f32[256,256]{1,0:T(8,128)} %reduce_sum.48) | copy-start | bytes 786436
  515.7 245.6 %copy-start.3 = (f32[768,256]{1,0:T(8,128)}, f32[768,256]{1,0:T(8,128)S(1)}, u32[]{:S(2)}) copy-start(f32[768,256]{1,0:T(8,128)S(1)} %reduce_sum.46) | copy-start | bytes 2359300
  515.7 245.6 %slice-start = ((s8[4718592]{0:T(1024)(128)(4,1)}), s8[524288]{0:T(1024)(128)(4,1)S(1)}, s32[]{:S(2)}) async-start(s8[4718592]{0:T(1024)(128)(4,1)} %bitcast.75), calls=%async_computation.5 | async-start | bytes 1048576
  735.9 25.4 %slice-start.1 = ((s8[4718592]{0:T(1024)(128)(4,1)}), s8[4194304]{0:T(1024)(128)(4,1)S(1)}, s32[]{:S(2)}) async-start(s8[4718592]{0:T(1024)(128)(4,1)} %bitcast.75), calls=%async_computation.6 | async-start | bytes 8388608
  751.5 16.2 %copy-start.1 = (s32[16]{0:T(128)S(1)}, s32[16]{0:T(128)}, u32[]{:S(2)}) copy-start(s32[16]{0:T(128)} %param.15) | copy-start | bytes 196
Sparse Core Ops, SparseCore 0:
  14.3 240.0 all-gather.12
  328.2 54.2 all-gather.8
  384.6 127.6 all-gather.14
  513.9 52.7 all-gather.10
  568.7 167.0 all-gather.16
